TPU v7x, 32 devices: a whole 2x2x4 slice. The times are simulated.
32 devices in a mesh: row: 8 (over y, x, core), col: 4 (over z).
Axes of the slice: x: 2, y: 2, z: 4, core: 2. Of those that a mesh axis runs over, the one named last changes fastest.
Arguments:
- block_values: bfloat16 [8, 4, 64, 256, 256], P('row', 'col'), may hold values from -0.1875 to 0.1875
- block_rows: int32 [8, 4, 64], P('row', 'col'), may hold values from 0 to 63
- block_cols: int32 [8, 4, 64], P('row', 'col'), may hold values from 0 to 255
- live_count: int32 [8, 4], P('row', 'col'), may hold values from 16 to 64, as said below
- objective: float32 [262144], P('col'), may hold values from -6 to 6
- upper_bound: float32 [262144], P('col'), may hold values from 0.5 to 2
- demand: float32 [131072], P('row'), may hold values from -6 to 6
- primal_start: float32 [262144], P('col'), may hold values from 0 to 0.5
- dual_start: float32 [131072], P('row'), may hold values from 0 to 0.5
- restart_at: int32 [8], replicated, may hold values 0 or 1
Outputs:
- primal_final: float32 [262144], P('col')
- dual_final: float32 [131072], P('row')
Inputs may be any that keep to these rules, and one draw needn't show every extreme that they name: `live_count`: each device's count of used slots; some device uses all 64.
All inputs are finite; a program needn't handle non-finite values.
Results may differ from a plain program's by a relative error of at most 0.0018.
Values may be sent and summed in bfloat16 or wider, within the bound.
A program may use at most 64 MiB of HBM per device.

v0:
```python
import jax
import jax.numpy as jnp
from jax import lax
from jax.sharding import PartitionSpec as P

ITERS = 8
step_scale = 0.3
epsilon = 1e-06


def shards(
    block_values,
    block_rows,
    block_cols,
    live_count,
    objective,
    upper_bound,
    demand,
    primal_start,
    dual_start,
    restart_at,
):
    slot_values = block_values[0, 0]
    rows_index = block_rows[0, 0]
    cols_index = block_cols[0, 0]
    used_slots = live_count[0, 0]
    slots = slot_values.shape[0]
    block_size = slot_values.shape[1]
    row_blocks = demand.shape[0] // block_size
    col_blocks = objective.shape[0] // block_size
    row_count = lax.axis_size("row")
    col_count = lax.axis_size("col")
    row_rank = lax.axis_index("row")
    col_rank = lax.axis_index("col")
    total_cols = objective.shape[0] * col_count
    total_rows = demand.shape[0] * row_count
    share_len = objective.shape[0] // row_count
    dual_len = demand.shape[0] // col_count
    live_slot = jnp.arange(slots, dtype=jnp.int32) < used_slots
    row_onehot = (
        (rows_index[:, None] == jnp.arange(row_blocks, dtype=jnp.int32)[None, :])
        & live_slot[:, None]
    ).astype(jnp.float32)
    col_onehot = (
        (cols_index[:, None] == jnp.arange(col_blocks, dtype=jnp.int32)[None, :])
        & live_slot[:, None]
    ).astype(jnp.float32)
    x = primal_start
    y = dual_start
    anchor_x = x
    anchor_y = y
    sum_x = jnp.zeros_like(x)
    sum_y = jnp.zeros_like(y)
    taken = jnp.zeros((), jnp.float32)
    omega = jnp.ones((), jnp.float32)
    for k in range(ITERS):
        step_primal = step_scale / omega
        step_dual = step_scale * omega
        y_low = y.astype(jnp.bfloat16)
        dual_pieces = y_low.reshape(row_blocks, block_size)[rows_index]
        dual_products = jnp.einsum(
            "tij,ti->tj", slot_values, dual_pieces, preferred_element_type=jnp.float32
        )
        dual_image = lax.psum(
            jnp.einsum(
                "tc,tj->cj", col_onehot, dual_products, precision=lax.Precision.HIGHEST
            ).reshape(-1),
            "row",
        )
        x_next = jnp.minimum(
            jnp.maximum(x - step_primal * (objective - dual_image), 0.0), upper_bound
        )
        extrap_low = (2.0 * x_next - x).astype(jnp.bfloat16)
        pieces = extrap_low.reshape(col_blocks, block_size)[cols_index]
        products = jnp.einsum("tij,tj->ti", slot_values, pieces, preferred_element_type=jnp.float32)
        primal_image = lax.psum(
            jnp.einsum("tr,ti->ri", row_onehot, products, precision=lax.Precision.HIGHEST).reshape(
                -1
            ),
            "col",
        )
        y_next = jnp.maximum(y + step_dual * (demand - primal_image), 0.0)
        x = x_next
        y = y_next
        sum_x = sum_x + x
        sum_y = sum_y + y
        taken = taken + 1.0
        if k <= ITERS - 3:
            is_restart = restart_at[k] == 1
            mean_x = sum_x / taken
            mean_y = sum_y / taken
            gap_x = lax.dynamic_slice_in_dim(mean_x - anchor_x, row_rank * share_len, share_len)
            gap_y = lax.dynamic_slice_in_dim(mean_y - anchor_y, col_rank * dual_len, dual_len)
            square_x = lax.psum(jnp.sum(gap_x * gap_x), ("row", "col"))
            square_y = lax.psum(jnp.sum(gap_y * gap_y), ("row", "col"))
            drift_x = square_x / total_cols + epsilon
            drift_y = square_y / total_rows + epsilon
            omega_next = jnp.sqrt(omega) * (drift_x / drift_y) ** 0.25
            x = jnp.where(is_restart, mean_x, x)
            y = jnp.where(is_restart, mean_y, y)
            anchor_x = jnp.where(is_restart, mean_x, anchor_x)
            anchor_y = jnp.where(is_restart, mean_y, anchor_y)
            sum_x = jnp.where(is_restart, jnp.zeros_like(sum_x), sum_x)
            sum_y = jnp.where(is_restart, jnp.zeros_like(sum_y), sum_y)
            taken = jnp.where(is_restart, jnp.zeros_like(taken), taken)
            omega = jnp.where(is_restart, omega_next, omega)
    return (x, y)


def solution(mesh):
    placed = (
        P("row", "col", None, None, None),
        P("row", "col", None),
        P("row", "col", None),
        P("row", "col"),
        P("col"),
        P("col"),
        P("row"),
        P("col"),
        P("row"),
        P(),
    )
    return jax.shard_map(
        shards, mesh=mesh, in_specs=placed, out_specs=(P("col"), P("row")), check_vma=False
    )
```

profile of v0, /device:TPU:0, one launch (start us, length us, event | category | flops | bytes accessed | tf_op | source)
XLA Modules:
  0.0 848.5 jit_solution(4290460746907200810)
XLA Ops:
  10.1 4.6 fusion.30
  16.1 56.7 %all-reduce.23.cloned.1.call-done = f32[65536]{0:T(1024)} async-done(((f32[65536]{0:T(1024)}), f32[65536]{0:T(1024)}) %all-reduce.23.cloned.1.call-update) | async-done | bytes 262160 | tf_op jit(solution)/shard_map/psum | solution.py:64
  74.6 5.6 fusion.28
  81.3 33.8 %all-reduce.25.cloned.1.call-done = f32[16384]{0:T(1024)} async-done(((f32[16384]{0:T(1024)}), f32[16384]{0:T(1024)}) %all-reduce.25.cloned.1.call-update) | async-done | bytes 65552 | tf_op jit(solution)/shard_map/psum | solution.py:76
  116.7 4.6 fusion.26
  125.9 40.4 %all-reduce.5 = (f32[]{:T(128)}, f32[]{:T(128)}) all-reduce(f32[]{:T(128)} %fusion.98, f32[]{:T(128)} %fusion.138), channel_id=1, replica_groups=mesh['row'=8,'col'=4] {'row','col'}, use_global_device_ids=true, to_apply=%region_2.0 | all-reduce | flops 2 | bytes 16 | tf_op jit(solution)/shard_map/psum | solution.py:94
  167.7 8.6 %all-reduce.27.cloned.1.call-done = f32[65536]{0:T(1024)} async-done(((f32[65536]{0:T(1024)}), f32[65536]{0:T(1024)}) %all-reduce.27.cloned.1.call-update) | async-done | bytes 262160 | tf_op jit(solution)/shard_map/psum | solution.py:64
  178.1 5.6 fusion.24
  184.8 33.8 %all-reduce.29.cloned.1.call-done = f32[16384]{0:T(1024)} async-done(((f32[16384]{0:T(1024)}), f32[16384]{0:T(1024)}) %all-reduce.29.cloned.1.call-update) | async-done | bytes 65552 | tf_op jit(solution)/shard_map/psum | solution.py:76
  227.5 40.3 %all-reduce.4 = (f32[]{:T(128)}, f32[]{:T(128)}) all-reduce(f32[]{:T(128)} %fusion.96, f32[]{:T(128)} %fusion.136), channel_id=1, replica_groups=mesh['row'=8,'col'=4] {'row','col'}, use_global_device_ids=true, to_apply=%region_8.9 | all-reduce | flops 2 | bytes 16 | tf_op jit(solution)/shard_map/psum | solution.py:94
  269.3 10.5 %all-reduce.31.cloned.1.call-done = f32[65536]{0:T(1024)} async-done(((f32[65536]{0:T(1024)}), f32[65536]{0:T(1024)}) %all-reduce.31.cloned.1.call-update) | async-done | bytes 262160 | tf_op jit(solution)/shard_map/psum | solution.py:64
  281.7 5.6 fusion.20
  289.3 32.9 %all-reduce.33.cloned.1.call-done = f32[16384]{0:T(1024)} async-done(((f32[16384]{0:T(1024)}), f32[16384]{0:T(1024)}) %all-reduce.33.cloned.1.call-update) | async-done | bytes 65552 | tf_op jit(solution)/shard_map/psum | solution.py:76
  331.5 40.3 %all-reduce.3 = (f32[]{:T(128)}, f32[]{:T(128)}) all-reduce(f32[]{:T(128)} %fusion.94, f32[]{:T(128)} %fusion.134), channel_id=1, replica_groups=mesh['row'=8,'col'=4] {'row','col'}, use_global_device_ids=true, to_apply=%region_14.15 | all-reduce | flops 2 | bytes 16 | tf_op jit(solution)/shard_map/psum | solution.py:94
  373.1 10.3 %all-reduce.35.cloned.1.call-done = f32[65536]{0:T(1024)} async-done(((f32[65536]{0:T(1024)}), f32[65536]{0:T(1024)}) %all-reduce.35.cloned.1.call-update) | async-done | bytes 262160 | tf_op jit(solution)/shard_map/psum | solution.py:64
  385.2 5.6 fusion.16
  391.9 33.8 %all-reduce.37.cloned.1.call-done = f32[16384]{0:T(1024)} async-done(((f32[16384]{0:T(1024)}), f32[16384]{0:T(1024)}) %all-reduce.37.cloned.1.call-update) | async-done | bytes 65552 | tf_op jit(solution)/shard_map/psum | solution.py:76
  434.5 40.3 %all-reduce.2 = (f32[]{:T(128)}, f32[]{:T(128)}) all-reduce(f32[]{:T(128)} %fusion.92, f32[]{:T(128)} %fusion.132), channel_id=1, replica_groups=mesh['row'=8,'col'=4] {'row','col'}, use_global_device_ids=true, to_apply=%region_20.21 | all-reduce | flops 2 | bytes 16 | tf_op jit(solution)/shard_map/psum | solution.py:94
  476.1 10.8 %all-reduce.39.cloned.1.call-done = f32[65536]{0:T(1024)} async-done(((f32[65536]{0:T(1024)}), f32[65536]{0:T(1024)}) %all-reduce.39.cloned.1.call-update) | async-done | bytes 262160 | tf_op jit(solution)/shard_map/psum | solution.py:64
  488.8 5.6 fusion.12
  496.2 33.2 %all-reduce.41.cloned.1.call-done = f32[16384]{0:T(1024)} async-done(((f32[16384]{0:T(1024)}), f32[16384]{0:T(1024)}) %all-reduce.41.cloned.1.call-update) | async-done | bytes 65552 | tf_op jit(solution)/shard_map/psum | solution.py:76
  538.1 40.3 %all-reduce.1 = (f32[]{:T(128)}, f32[]{:T(128)}) all-reduce(f32[]{:T(128)} %multiply_reduce_fusion, f32[]{:T(128)} %multiply_reduce_fusion.1), channel_id=1, replica_groups=mesh['row'=8,'col'=4] {'row','col'}, use_global_device_ids=true, to_apply=%region_26.27 | all-reduce | flops 2 | bytes 16 | tf_op jit(solution)/shard_map/psum | solution.py:94
  579.9 10.7 %all-reduce.43.cloned.1.call-done = f32[65536]{0:T(1024)} async-done(((f32[65536]{0:T(1024)}), f32[65536]{0:T(1024)}) %all-reduce.43.cloned.1.call-update) | async-done | bytes 262160 | tf_op jit(solution)/shard_map/psum | solution.py:64
  592.4 5.6 fusion.8
  600.0 33.0 %all-reduce.45.cloned.1.call-done = f32[16384]{0:T(1024)} async-done(((f32[16384]{0:T(1024)}), f32[16384]{0:T(1024)}) %all-reduce.45.cloned.1.call-update) | async-done | bytes 65552 | tf_op jit(solution)/shard_map/psum | solution.py:76
  641.7 40.4 %all-reduce = (f32[]{:T(128)}, f32[]{:T(128)}) all-reduce(f32[]{:T(128)} %fusion.90, f32[]{:T(128)} %fusion.130), channel_id=1, replica_groups=mesh['row'=8,'col'=4] {'row','col'}, use_global_device_ids=true, to_apply=%region_32.33 | all-reduce | flops 2 | bytes 16 | tf_op jit(solution)/shard_map/psum | solution.py:94
  683.5 10.6 %all-reduce.47.cloned.1.call-done = f32[65536]{0:T(1024)} async-done(((f32[65536]{0:T(1024)}), f32[65536]{0:T(1024)}) %all-reduce.47.cloned.1.call-update) | async-done | bytes 262160 | tf_op jit(solution)/shard_map/psum | solution.py:64
  695.9 5.6 fusion.4
  702.6 33.8 %all-reduce.49.cloned.1.call-done = f32[16384]{0:T(1024)} async-done(((f32[16384]{0:T(1024)}), f32[16384]{0:T(1024)}) %all-reduce.49.cloned.1.call-update) | async-done | bytes 65552 | tf_op jit(solution)/shard_map/psum | solution.py:76
  743.9 53.7 %all-reduce.51.cloned.1.call-done = f32[65536]{0:T(1024)} async-done(((f32[65536]{0:T(1024)}), f32[65536]{0:T(1024)}) %all-reduce.51.cloned.1.call-update) | async-done | bytes 262160 | tf_op jit(solution)/shard_map/psum | solution.py:64
  800.0 5.6 fusion
  806.7 33.8 %all-reduce.53.cloned.1.call-done = f32[16384]{0:T(1024)} async-done(((f32[16384]{0:T(1024)}), f32[16384]{0:T(1024)}) %all-reduce.53.cloned.1.call-update) | async-done | bytes 65552 | tf_op jit(solution)/shard_map/psum | solution.py:76
  (160 shorter events, 84.7 us)
Async XLA Ops:
  7.2 7.6 copy-start.5
  7.2 65.6 %all-reduce.23.cloned.1.call-start = ((), (), s32[]{:S(2)}) async-start(), calls=%async_computation | async-start | bytes 524288 | tf_op jit(solution)/shard_map/psum | solution.py:64
  10.1 62.7 %copy-start = (f32[65536]{0:T(1024)S(1)}, f32[65536]{0:T(1024)}, u32[]{:S(2)}) copy-start(f32[65536]{0:T(1024)} %param.15) | copy-start | bytes 786436
  10.1 62.7 %copy-start.1 = (f32[65536]{0:T(1024)S(1)}, f32[65536]{0:T(1024)}, u32[]{:S(2)}) copy-start(f32[65536]{0:T(1024)} %param.14) | copy-start | bytes 786436
  10.1 62.7 %copy-start.3 = (f32[65536]{0:T(1024)S(1)}, f32[65536]{0:T(1024)}, u32[]{:S(2)}) copy-start(f32[65536]{0:T(1024)} %param.17) | copy-start | bytes 786436
  14.8 65.4 %copy-start.6 = (s32[1,1,64]{2,1,0:T(1,128)S(1)}, s32[1,1,64]{2,1,0:T(1,128)}, u32[]{:S(2)}) copy-start(s32[1,1,64]{2,1,0:T(1,128)} %param.11) | copy-start | bytes 772
  14.8 100.3 %copy-start.2 = (f32[16384]{0:T(1024)S(1)}, f32[16384]{0:T(1024)}, u32[]{:S(2)}) copy-start(f32[16384]{0:T(1024)} %param.16) | copy-start | bytes 196612
  14.8 100.3 %copy-start.4 = (f32[16384]{0:T(1024)S(1)}, f32[16384]{0:T(1024)}, u32[]{:S(2)}) copy-start(f32[16384]{0:T(1024)} %param.18) | copy-start | bytes 196612
  16.1 99.0 %all-reduce.25.cloned.1.call-start = ((), (), s32[]{:S(2)}) async-start(), calls=%async_computation.1 | async-start | bytes 131072 | tf_op jit(solution)/shard_map/psum | solution.py:76
  81.2 95.0 %all-reduce.27.cloned.1.call-start = ((), (), s32[]{:S(2)}) async-start(), calls=%async_computation.2 | async-start | bytes 524288 | tf_op jit(solution)/shard_map/psum | solution.py:64
  116.7 5.9 copy-start.7
  122.5 96.1 %all-reduce.29.cloned.1.call-start = ((), (), s32[]{:S(2)}) async-start(), calls=%async_computation.3 | async-start | bytes 131072 | tf_op jit(solution)/shard_map/psum | solution.py:76
  184.8 95.1 %all-reduce.31.cloned.1.call-start = ((), (), s32[]{:S(2)}) async-start(), calls=%async_computation.4 | async-start | bytes 524288 | tf_op jit(solution)/shard_map/psum | solution.py:64
  226.1 96.1 %all-reduce.33.cloned.1.call-start = ((), (), s32[]{:S(2)}) async-start(), calls=%async_computation.5 | async-start | bytes 131072 | tf_op jit(solution)/shard_map/psum | solution.py:76
  288.3 95.1 %all-reduce.35.cloned.1.call-start = ((), (), s32[]{:S(2)}) async-start(), calls=%async_computation.6 | async-start | bytes 524288 | tf_op jit(solution)/shard_map/psum | solution.py:64
  329.6 96.1 %all-reduce.37.cloned.1.call-start = ((), (), s32[]{:S(2)}) async-start(), calls=%async_computation.7 | async-start | bytes 131072 | tf_op jit(solution)/shard_map/psum | solution.py:76
  391.9 95.1 %all-reduce.39.cloned.1.call-start = ((), (), s32[]{:S(2)}) async-start(), calls=%async_computation.8 | async-start | bytes 524288 | tf_op jit(solution)/shard_map/psum | solution.py:64
  433.2 96.1 %all-reduce.41.cloned.1.call-start = ((), (), s32[]{:S(2)}) async-start(), calls=%async_computation.9 | async-start | bytes 131072 | tf_op jit(solution)/shard_map/psum | solution.py:76
  495.5 95.1 %all-reduce.43.cloned.1.call-start = ((), (), s32[]{:S(2)}) async-start(), calls=%async_computation.10 | async-start | bytes 524288 | tf_op jit(solution)/shard_map/psum | solution.py:64
  536.8 96.1 %all-reduce.45.cloned.1.call-start = ((), (), s32[]{:S(2)}) async-start(), calls=%async_computation.11 | async-start | bytes 131072 | tf_op jit(solution)/shard_map/psum | solution.py:76
  599.1 95.0 %all-reduce.47.cloned.1.call-start = ((), (), s32[]{:S(2)}) async-start(), calls=%async_computation.12 | async-start | bytes 524288 | tf_op jit(solution)/shard_map/psum | solution.py:64
  640.4 96.0 %all-reduce.49.cloned.1.call-start = ((), (), s32[]{:S(2)}) async-start(), calls=%async_computation.13 | async-start | bytes 131072 | tf_op jit(solution)/shard_map/psum | solution.py:76
  702.5 95.0 %all-reduce.51.cloned.1.call-start = ((), (), s32[]{:S(2)}) async-start(), calls=%async_computation.14 | async-start | bytes 524288 | tf_op jit(solution)/shard_map/psum | solution.py:64
  743.8 96.7 %all-reduce.53.cloned.1.call-start = ((), (), s32[]{:S(2)}) async-start(), calls=%async_computation.15 | async-start | bytes 131072 | tf_op jit(solution)/shard_map/psum | solution.py:76
Sparse Core Ops, SparseCore 0:
  16.2 56.5 all-reduce.22
  81.4 33.6 all-reduce.24
  122.7 53.5 all-reduce.26
  184.9 33.6 all-reduce.28
  226.2 53.5 all-reduce.30
  288.5 33.7 all-reduce.32
  329.8 53.5 all-reduce.34
  392.0 33.6 all-reduce.36
  433.3 53.6 all-reduce.38
  495.6 33.6 all-reduce.40
  536.9 53.6 all-reduce.42
  599.2 33.6 all-reduce.44
  640.5 53.5 all-reduce.46
  702.7 33.6 all-reduce.48
  743.9 53.5 all-reduce.50
  806.8 33.6 all-reduce.52
where the time goes:
time: 850 us; the launch traced here: 849 us
  waiting for transfers between devices  440 us (52%)
  blocking collectives  242 us (28%)
  matrix products  87.5 us (10%)
  between operations  27.6 us (3%)
  other arithmetic  25.7 us (3%)
  local copies, waits for them, and re-layouts  24.5 us (3%)
    psum x8, waiting for transfers between devices, shards(): lax.psum(jnp.einsum('tr,ti->ri', row_onehot, products, precision=lax.Prec...  268 us
    psum x6, blocking collectives, shards(): square_x = lax.psum(jnp.sum(gap_x * gap_x), ('row', 'col'))  242 us
    psum x8, waiting for transfers between devices, shards(): lax.psum(jnp.einsum('tc,tj->cj', col_onehot, dual_products, precision=lax...  172 us
    dot_general x8, matrix products, shards(): jnp.einsum('tij,tj->ti', slot_values, pieces, preferred_element_type=jnp....  45.1 us
    dot_general x8, matrix products, shards(): jnp.einsum('tij,ti->tj', slot_values, dual_pieces, preferred_element_type...  36.7 us
  transfers between devices with their start and end apart: 16, of which 16 were waited for; matrix products, arithmetic and copies ran while one was open for 1% of the time, Pallas kernels for 0%

commit v1 on v0

--- a/solution.py
+++ b/solution.py
@@ -61,11 +61,14 @@
         dual_products = jnp.einsum(
             "tij,ti->tj", slot_values, dual_pieces, preferred_element_type=jnp.float32
         )
-        dual_image = lax.psum(
-            jnp.einsum(
-                "tc,tj->cj", col_onehot, dual_products, precision=lax.Precision.HIGHEST
-            ).reshape(-1),
-            "row",
+        dual_image = jnp.sum(
+            lax.all_gather(
+                jnp.einsum(
+                    "tc,tj->cj", col_onehot, dual_products, precision=lax.Precision.HIGHEST
+                ).reshape(-1),
+                "row",
+            ),
+            axis=0,
         )
         x_next = jnp.minimum(
             jnp.maximum(x - step_primal * (objective - dual_image), 0.0), upper_bound

time: 850 us -> 767 us (0.902)
  waiting for transfers between devices: 440 us -> 330 us
  other arithmetic: 25.7 us -> 43.1 us
    psum x8 -> x0, waiting for transfers between devices: 172 us -> none  [shards(): lax.psum(jnp.einsum('tc,tj->cj', col_onehot, dual_products, precision=lax...]
    all_gather x0 -> x8, waiting for transfers between devices: none -> 58.3 us  [shards(): lax.all_gather(jnp.einsum('tc,tj->cj', col_onehot, dual_products, precisi...]
    reduce_sum x0 -> x8, other arithmetic: none -> 25 us  [shards(): jnp.sum(lax.all_gather(jnp.einsum('tc,tj->cj', col_onehot, dual_products,...]
  transfers between devices with their start and end apart: 16 -> 16, of which waited for: 16 -> 10; matrix products, arithmetic and copies ran while one was open for 1% -> 1% of each run, Pallas kernels for 0% -> 0%
where the time goes in v1:
time: 767 us; the launch traced here: 758 us
  waiting for transfers between devices  330 us (43%)
  blocking collectives  242 us (32%)
  matrix products  87.5 us (11%)
  other arithmetic  43.1 us (6%)
  between operations  27.8 us (4%)
  local copies, waits for them, and re-layouts  25.5 us (3%)
    psum x8, waiting for transfers between devices, shards(): lax.psum(jnp.einsum('tr,ti->ri', row_onehot, products, precision=lax.Prec...  272 us
    psum x6, blocking collectives, shards(): square_x = lax.psum(jnp.sum(gap_x * gap_x), ('row', 'col'))  242 us
    all_gather x8, waiting for transfers between devices, shards(): lax.all_gather(jnp.einsum('tc,tj->cj', col_onehot, dual_products, precisi...  58.3 us
    dot_general x8, matrix products, shards(): jnp.einsum('tij,tj->ti', slot_values, pieces, preferred_element_type=jnp....  45.1 us
    dot_general x8, matrix products, shards(): jnp.einsum('tij,ti->tj', slot_values, dual_pieces, preferred_element_type...  36.7 us
    reduce_sum x8, other arithmetic, shards(): jnp.sum(lax.all_gather(jnp.einsum('tc,tj->cj', col_onehot, dual_products,...  25 us
  transfers between devices with their start and end apart: 16, of which 10 were waited for; matrix products, arithmetic and copies ran while one was open for 1% of the time, Pallas kernels for 0%

profile of v1, /device:TPU:0, one launch (start us, length us, event | category | flops | bytes accessed | tf_op | source)
XLA Modules:
  0.0 757.6 jit_solution(10503436677816793574)
XLA Ops:
  10.1 4.6 fusion.30
  16.3 30.6 %all-gather.17.cloned.1.call-done = f32[8,1,65536]{2,1,0:T(1,128)} async-done(((f32[1,1,65536]{2,1,0:T(1,128)}), f32[8,1,65536]{2,1,0:T(1,128)}) %all-gather.17.cloned.1.call-update) | async-done | bytes 2097168 | tf_op jit(solution)/shard_map/all_gather | solution.py:65
  50.8 5.6 fusion.28
  57.5 34.4 %all-reduce.15.cloned.1.call-done = f32[16384]{0:T(1024)} async-done(((f32[16384]{0:T(1024)}), f32[16384]{0:T(1024)}) %all-reduce.15.cloned.1.call-update) | async-done | bytes 65552 | tf_op jit(solution)/shard_map/psum | solution.py:79
  93.6 4.6 fusion.26
  102.7 40.3 %all-reduce.5 = (f32[]{:T(128)}, f32[]{:T(128)}) all-reduce(f32[]{:T(128)} %fusion.106, f32[]{:T(128)} %fusion.146), channel_id=1, replica_groups=mesh['row'=8,'col'=4] {'row','col'}, use_global_device_ids=true, to_apply=%region_2.0 | all-reduce | flops 2 | bytes 16 | tf_op jit(solution)/shard_map/psum | solution.py:97
  148.6 5.6 fusion.24
  155.8 33.8 %all-reduce.17.cloned.1.call-done = f32[16384]{0:T(1024)} async-done(((f32[16384]{0:T(1024)}), f32[16384]{0:T(1024)}) %all-reduce.17.cloned.1.call-update) | async-done | bytes 65552 | tf_op jit(solution)/shard_map/psum | solution.py:79
  191.2 4.6 fusion.22
  198.4 40.3 %all-reduce.4 = (f32[]{:T(128)}, f32[]{:T(128)}) all-reduce(f32[]{:T(128)} %fusion.104, f32[]{:T(128)} %fusion.144), channel_id=1, replica_groups=mesh['row'=8,'col'=4] {'row','col'}, use_global_device_ids=true, to_apply=%region_8.9 | all-reduce | flops 2 | bytes 16 | tf_op jit(solution)/shard_map/psum | solution.py:97
  244.1 5.6 fusion.20
  251.5 33.7 %all-reduce.19.cloned.1.call-done = f32[16384]{0:T(1024)} async-done(((f32[16384]{0:T(1024)}), f32[16384]{0:T(1024)}) %all-reduce.19.cloned.1.call-update) | async-done | bytes 65552 | tf_op jit(solution)/shard_map/psum | solution.py:79
  286.7 4.6 fusion.18
  294.7 40.5 %all-reduce.3 = (f32[]{:T(128)}, f32[]{:T(128)}) all-reduce(f32[]{:T(128)} %fusion.102, f32[]{:T(128)} %fusion.142), channel_id=1, replica_groups=mesh['row'=8,'col'=4] {'row','col'}, use_global_device_ids=true, to_apply=%region_14.15 | all-reduce | flops 2 | bytes 16 | tf_op jit(solution)/shard_map/psum | solution.py:97
  340.6 5.6 fusion.16
  347.5 33.9 %all-reduce.21.cloned.1.call-done = f32[16384]{0:T(1024)} async-done(((f32[16384]{0:T(1024)}), f32[16384]{0:T(1024)}) %all-reduce.21.cloned.1.call-update) | async-done | bytes 65552 | tf_op jit(solution)/shard_map/psum | solution.py:79
  383.0 4.6 fusion.14
  390.3 40.3 %all-reduce.2 = (f32[]{:T(128)}, f32[]{:T(128)}) all-reduce(f32[]{:T(128)} %fusion.100, f32[]{:T(128)} %fusion.140), channel_id=1, replica_groups=mesh['row'=8,'col'=4] {'row','col'}, use_global_device_ids=true, to_apply=%region_20.21 | all-reduce | flops 2 | bytes 16 | tf_op jit(solution)/shard_map/psum | solution.py:97
  436.1 5.6 fusion.12
  443.4 33.7 %all-reduce.23.cloned.1.call-done = f32[16384]{0:T(1024)} async-done(((f32[16384]{0:T(1024)}), f32[16384]{0:T(1024)}) %all-reduce.23.cloned.1.call-update) | async-done | bytes 65552 | tf_op jit(solution)/shard_map/psum | solution.py:79
  478.7 4.6 fusion.10
  486.0 40.3 %all-reduce.1 = (f32[]{:T(128)}, f32[]{:T(128)}) all-reduce(f32[]{:T(128)} %multiply_reduce_fusion, f32[]{:T(128)} %multiply_reduce_fusion.1), channel_id=1, replica_groups=mesh['row'=8,'col'=4] {'row','col'}, use_global_device_ids=true, to_apply=%region_26.27 | all-reduce | flops 2 | bytes 16 | tf_op jit(solution)/shard_map/psum | solution.py:97
  531.8 5.6 fusion.8
  539.3 33.5 %all-reduce.25.cloned.1.call-done = f32[16384]{0:T(1024)} async-done(((f32[16384]{0:T(1024)}), f32[16384]{0:T(1024)}) %all-reduce.25.cloned.1.call-update) | async-done | bytes 65552 | tf_op jit(solution)/shard_map/psum | solution.py:79
  574.4 4.6 fusion.6
  581.7 40.3 %all-reduce = (f32[]{:T(128)}, f32[]{:T(128)}) all-reduce(f32[]{:T(128)} %fusion.98, f32[]{:T(128)} %fusion.138), channel_id=1, replica_groups=mesh['row'=8,'col'=4] {'row','col'}, use_global_device_ids=true, to_apply=%region_32.33 | all-reduce | flops 2 | bytes 16 | tf_op jit(solution)/shard_map/psum | solution.py:97
  627.4 5.6 fusion.4
  634.1 34.3 %all-reduce.27.cloned.1.call-done = f32[16384]{0:T(1024)} async-done(((f32[16384]{0:T(1024)}), f32[16384]{0:T(1024)}) %all-reduce.27.cloned.1.call-update) | async-done | bytes 65552 | tf_op jit(solution)/shard_map/psum | solution.py:79
  670.0 4.6 fusion.2
  676.0 27.6 %all-gather.31.cloned.1.call-done = f32[8,1,65536]{2,1,0:T(1,128)} async-done(((f32[1,1,65536]{2,1,0:T(1,128)}), f32[8,1,65536]{2,1,0:T(1,128)}) %all-gather.31.cloned.1.call-update) | async-done | bytes 2097168 | tf_op jit(solution)/shard_map/all_gather | solution.py:65
  708.3 5.6 fusion
  714.9 34.5 %all-reduce.29.cloned.1.call-done = f32[16384]{0:T(1024)} async-done(((f32[16384]{0:T(1024)}), f32[16384]{0:T(1024)}) %all-reduce.29.cloned.1.call-update) | async-done | bytes 65552 | tf_op jit(solution)/shard_map/psum | solution.py:79
  (168 shorter events, 76.2 us)
Async XLA Ops:
  7.2 7.6 %copy-start.5 = (s32[1,1,64]{2,1,0:T(1,128)S(1)}, s32[1,1,64]{2,1,0:T(1,128)}, u32[]{:S(2)}) copy-start(s32[1,1,64]{2,1,0:T(1,128)} %param.12) | copy-start | bytes 772
  7.2 39.7 %all-gather.17.cloned.1.call-start = ((), (), s32[]{:S(2)}) async-start(), calls=%async_computation.8 | async-start | bytes 2359296 | tf_op jit(solution)/shard_map/all_gather | solution.py:65
  10.1 39.9 %copy-start = (f32[65536]{0:T(1024)S(1)}, f32[65536]{0:T(1024)}, u32[]{:S(2)}) copy-start(f32[65536]{0:T(1024)} %param.15) | copy-start | bytes 786436
  10.1 39.9 %copy-start.1 = (f32[65536]{0:T(1024)S(1)}, f32[65536]{0:T(1024)}, u32[]{:S(2)}) copy-start(f32[65536]{0:T(1024)} %param.14) | copy-start | bytes 786436
  10.1 39.9 %copy-start.3 = (f32[65536]{0:T(1024)S(1)}, f32[65536]{0:T(1024)}, u32[]{:S(2)}) copy-start(f32[65536]{0:T(1024)} %param.17) | copy-start | bytes 786436
  14.8 41.7 %copy-start.6 = (s32[1,1,64]{2,1,0:T(1,128)S(1)}, s32[1,1,64]{2,1,0:T(1,128)}, u32[]{:S(2)}) copy-start(s32[1,1,64]{2,1,0:T(1,128)} %param.11) | copy-start | bytes 772
  14.8 77.2 %copy-start.2 = (f32[16384]{0:T(1024)S(1)}, f32[16384]{0:T(1024)}, u32[]{:S(2)}) copy-start(f32[16384]{0:T(1024)} %param.16) | copy-start | bytes 196612
  14.8 77.2 %copy-start.4 = (f32[16384]{0:T(1024)S(1)}, f32[16384]{0:T(1024)}, u32[]{:S(2)}) copy-start(f32[16384]{0:T(1024)} %param.18) | copy-start | bytes 196612
  16.2 75.8 %all-reduce.15.cloned.1.call-start = ((), (), s32[]{:S(2)}) async-start(), calls=%async_computation | async-start | bytes 131072 | tf_op jit(solution)/shard_map/psum | solution.py:79
  57.5 87.1 %all-gather.19.cloned.1.call-start = ((), (), s32[]{:S(2)}) async-start(), calls=%async_computation.9 | async-start | bytes 2359296 | tf_op jit(solution)/shard_map/all_gather | solution.py:65
  93.5 6.0 copy-start.7
  99.5 90.0 %all-reduce.17.cloned.1.call-start = ((), (), s32[]{:S(2)}) async-start(), calls=%async_computation.1 | async-start | bytes 131072 | tf_op jit(solution)/shard_map/psum | solution.py:79
  155.2 84.9 %all-gather.21.cloned.1.call-start = ((), (), s32[]{:S(2)}) async-start(), calls=%async_computation.10 | async-start | bytes 2359296 | tf_op jit(solution)/shard_map/all_gather | solution.py:65
  197.1 88.0 %all-reduce.19.cloned.1.call-start = ((), (), s32[]{:S(2)}) async-start(), calls=%async_computation.2 | async-start | bytes 131072 | tf_op jit(solution)/shard_map/psum | solution.py:79
  250.8 85.8 %all-gather.23.cloned.1.call-start = ((), (), s32[]{:S(2)}) async-start(), calls=%async_computation.11 | async-start | bytes 2359296 | tf_op jit(solution)/shard_map/all_gather | solution.py:65
  292.7 88.7 %all-reduce.21.cloned.1.call-start = ((), (), s32[]{:S(2)}) async-start(), calls=%async_computation.3 | async-start | bytes 131072 | tf_op jit(solution)/shard_map/psum | solution.py:79
  347.2 84.8 %all-gather.25.cloned.1.call-start = ((), (), s32[]{:S(2)}) async-start(), calls=%async_computation.12 | async-start | bytes 2359296 | tf_op jit(solution)/shard_map/all_gather | solution.py:65
  389.0 88.1 %all-reduce.23.cloned.1.call-start = ((), (), s32[]{:S(2)}) async-start(), calls=%async_computation.4 | async-start | bytes 131072 | tf_op jit(solution)/shard_map/psum | solution.py:79
  442.8 85.0 %all-gather.27.cloned.1.call-start = ((), (), s32[]{:S(2)}) async-start(), calls=%async_computation.13 | async-start | bytes 2359296 | tf_op jit(solution)/shard_map/all_gather | solution.py:65
  484.7 88.1 %all-reduce.25.cloned.1.call-start = ((), (), s32[]{:S(2)}) async-start(), calls=%async_computation.5 | async-start | bytes 131072 | tf_op jit(solution)/shard_map/psum | solution.py:79
  538.5 85.0 %all-gather.29.cloned.1.call-start = ((), (), s32[]{:S(2)}) async-start(), calls=%async_computation.14 | async-start | bytes 2359296 | tf_op jit(solution)/shard_map/all_gather | solution.py:65
  580.4 88.0 %all-reduce.27.cloned.1.call-start = ((), (), s32[]{:S(2)}) async-start(), calls=%async_computation.6 | async-start | bytes 131072 | tf_op jit(solution)/shard_map/psum | solution.py:79
  634.1 69.5 %all-gather.31.cloned.1.call-start = ((), (), s32[]{:S(2)}) async-start(), calls=%async_computation.15 | async-start | bytes 2359296 | tf_op jit(solution)/shard_map/all_gather | solution.py:65
  676.0 73.4 %all-reduce.29.cloned.1.call-start = ((), (), s32[]{:S(2)}) async-start(), calls=%async_computation.7 | async-start | bytes 131072 | tf_op jit(solution)/shard_map/psum | solution.py:79
Sparse Core Ops, SparseCore 0:
  16.3 30.4 all-gather.16
  57.6 34.2 all-reduce.14
  99.7 27.6 all-gather.18
  155.4 34.1 all-reduce.16
  197.3 27.6 all-gather.20
  250.9 34.1 all-reduce.18
  292.8 27.6 all-gather.22
  347.4 33.9 all-reduce.20
  389.1 27.6 all-gather.24
  442.9 34.1 all-reduce.22
  484.8 27.6 all-gather.26
  538.6 34.1 all-reduce.24
  580.5 27.6 all-gather.28
  634.2 34.1 all-reduce.26
  676.1 27.4 all-gather.30
  715.0 34.2 all-reduce.28
